TPU v7x, 512 devices: a whole 4x8x8 slice. The times are simulated.
512 devices in a mesh: expert: 32 (over y_lo, z, core), dp: 16 (over y_hi, x).
Axes of the slice: x: 4, y: 8 (y_hi: 4, y_lo: 2; y = y_hi * 2 + y_lo), z: 8, core: 2. Of those that a mesh axis runs over, the one named last changes fastest.
Arguments:
- tokens: bfloat16 [65536, 3584], P(('expert', 'dp')), may hold values from -6 to 6
- expert_ids: int32 [65536, 8], P(('expert', 'dp')), may hold values from 0 to 255, all different within a row
- gate_probs: float32 [65536, 8], P(('expert', 'dp')), may hold values from 0.02 to 0.5
- out_grad: bfloat16 [65536, 3584], P(('expert', 'dp')), may hold values from -6 to 6
- w_gate: bfloat16 [32, 1024, 3584], P('expert', 'dp'), may hold values from -0.09375 to 0.09375
- w_up: bfloat16 [32, 1024, 3584], P('expert', 'dp'), may hold values from -0.09375 to 0.09375
- w_down: bfloat16 [32, 1024, 3584], P('expert', 'dp'), may hold values from -0.1875 to 0.1875
Outputs:
- grad_gate: bfloat16 [32, 1024, 3584], P('expert', 'dp')
- grad_up: bfloat16 [32, 1024, 3584], P('expert', 'dp')
- grad_down: bfloat16 [32, 1024, 3584], P('expert', 'dp')
All inputs are finite; a program needn't handle non-finite values.
Results may differ from a plain program's by a relative error of at most 0.0058.
Values may be sent and summed in bfloat16 or wider, within the bound.
A program may use at most 64 MiB of HBM per device.

v0:
```python
import jax
import jax.numpy as jnp
from jax import lax
from jax.sharding import PartitionSpec as P

CAP = 2


def local_factors(rows_x, rows_dy, weight_gate, weight_up, weight_down):
    contract = (((1,), (1,)), ((), ()))
    gate_pre = lax.dot_general(rows_x, weight_gate, contract, preferred_element_type=jnp.float32)
    up_pre = lax.dot_general(rows_x, weight_up, contract, preferred_element_type=jnp.float32)
    back_grad = lax.dot_general(rows_dy, weight_down, contract, preferred_element_type=jnp.float32)
    sig_gate = jax.nn.sigmoid(gate_pre)
    act_gate = gate_pre * sig_gate
    hidden = (act_gate * up_pre).astype(jnp.bfloat16)
    d_gate = (back_grad * up_pre * sig_gate * (1.0 + gate_pre * (1.0 - sig_gate))).astype(
        jnp.bfloat16
    )
    d_up = (back_grad * act_gate).astype(jnp.bfloat16)
    return (d_gate, d_up, hidden)


def outer_sum(factor, rows):
    return lax.dot_general(
        factor, rows, (((0,), (0,)), ((), ())), preferred_element_type=jnp.float32
    )


def local(tokens, expert_ids, gate_probs, out_grad, w_gate, w_up, w_down):
    n_expert = lax.axis_size("expert")
    experts_all = w_gate.shape[0] * n_expert
    tok_rows, top_count = expert_ids.shape
    feature_count = tokens.shape[1]
    flat_ids = expert_ids.reshape(-1)
    expert_range = jnp.arange(experts_all, dtype=jnp.int32)
    onehot = (flat_ids[:, None] == expert_range[None, :]).astype(jnp.int32)
    before = jnp.cumsum(onehot, axis=0) - onehot
    slot_rank = jnp.sum(before * onehot, axis=1)
    kept_mask = (flat_ids < experts_all) & (slot_rank < CAP)
    slot_index = jnp.where(kept_mask, flat_ids * CAP + slot_rank, -1)
    slot_range = jnp.arange(experts_all * CAP, dtype=jnp.int32)
    matches = (slot_index[None, :] == slot_range[:, None]).astype(jnp.float32)
    matches = matches.reshape(experts_all * CAP, tok_rows, top_count)
    picker = jnp.sum(matches, axis=2).astype(jnp.bfloat16)
    slot_prob = jnp.sum(matches * gate_probs[None, :, :], axis=(1, 2))
    sent_x = jnp.dot(picker, tokens, preferred_element_type=jnp.float32).astype(jnp.bfloat16)
    sent_dy = (
        jnp.dot(picker, out_grad, preferred_element_type=jnp.float32) * slot_prob[:, None]
    ).astype(jnp.bfloat16)
    sent_x = sent_x.reshape(experts_all, CAP, feature_count)
    sent_dy = sent_dy.reshape(experts_all, CAP, feature_count)
    recv_x, recv_dy = (
        lax.all_to_all(sent_x, "expert", split_axis=0, concat_axis=0, tiled=True),
        lax.all_to_all(sent_dy, "expert", split_axis=0, concat_axis=0, tiled=True),
    )
    rows_x = recv_x.reshape(-1, feature_count)
    rows_dy = recv_dy.reshape(-1, feature_count)
    piece_x = lax.all_gather(rows_x, "dp", axis=0, tiled=True)
    piece_dy = lax.all_gather(rows_dy, "dp", axis=0, tiled=True)
    d_gate, d_up, hidden = local_factors(piece_x, piece_dy, w_gate[0], w_up[0], w_down[0])
    term_gate = outer_sum(d_gate, piece_x)
    term_up = outer_sum(d_up, piece_x)
    term_down = outer_sum(hidden, piece_dy)
    return (
        term_gate.astype(jnp.bfloat16)[None],
        term_up.astype(jnp.bfloat16)[None],
        term_down.astype(jnp.bfloat16)[None],
    )


def solution(mesh):
    in_specs = (
        P(("expert", "dp"), None),
        P(("expert", "dp"), None),
        P(("expert", "dp"), None),
        P(("expert", "dp"), None),
        P("expert", "dp", None),
        P("expert", "dp", None),
        P("expert", "dp", None),
    )
    out_specs = (P("expert", "dp", None), P("expert", "dp", None), P("expert", "dp", None))
    return jax.shard_map(local, mesh=mesh, in_specs=in_specs, out_specs=out_specs, check_vma=False)
```

profile of v0, /device:TPU:1, one launch (start us, length us, event | category | flops | bytes accessed | tf_op | source)
XLA Modules:
  0.0 293.1 jit_solution(2632505541616493926)
XLA Ops:
  7.2 0.0 copy-start
  7.2 0.0 copy-start.3
  7.2 0.0 all-gather.5.cloned.1.call-start
  7.2 0.9 copy.30
  8.1 0.1 eq.43
  8.2 0.1 eq.39
  8.3 9.0 %reduce-window.6 = s32[32,8,128]{2,1,0:T(8,128)S(1)} reduce-window(s32[32,8,128]{2,1,0:T(8,128)S(1)} %fusion.15, s32[]{:T(128)} %constant.4.clone.1), window={size=1x1x128 pad=0_0x0_0x127_0}, to_apply=%region_0.0 | reduce-window | flops 4161536 | bytes 262148 | tf_op jit(solution)/shard_map/reduce-window
  17.3 0.1 slice.8
  17.4 0.1 copy.32
  17.6 0.1 copy.33
  17.7 0.1 broadcast_add_fusion
  17.8 0.1 reduce_sum.30
  18.0 0.7 add_select_fusion
  18.7 1.2 select_reduce_fusion
  19.9 0.0 copy-done
  19.9 0.3 convolution_convert_fusion.3
  20.2 0.2 reshape.64
  20.4 27.1 %all_to_all.10 = bf16[32,2,3584]{2,1,0:T(2,128)(2,1)S(1)} all-to-all(bf16[32,2,3584]{2,1,0:T(2,128)(2,1)S(1)} %reshape.64), channel_id=1, replica_groups=mesh['expert'=32,'dp'=16] {'expert'}, dimensions={0} | all-to-all | bytes 917504 | tf_op jit(solution)/shard_map/all_to_all | solution.py:54
  47.5 0.0 copy-start.4
  47.5 0.9 reshape.65
  48.4 0.0 all-gather.5.cloned.1.call-update
  48.4 0.0 all-gather.3.cloned.1.call-start
  48.5 1.5 fusion
  49.9 0.2 reshape.62
  50.1 19.5 %all_to_all.11 = bf16[32,2,3584]{2,1,0:T(2,128)(2,1)S(1)} all-to-all(bf16[32,2,3584]{2,1,0:T(2,128)(2,1)S(1)} %reshape.62), channel_id=1, replica_groups=mesh['expert'=32,'dp'=16] {'expert'}, dimensions={0} | all-to-all | bytes 917504 | tf_op jit(solution)/shard_map/all_to_all | solution.py:55
  69.6 0.9 reshape.63
  70.6 0.0 all-gather.3.cloned.1.call-update
  70.6 0.0 copy-start.5
  70.6 85.9 %all-gather.5.cloned.1.call-done = bf16[1024,3584]{1,0:T(8,128)(2,1)} async-done(((bf16[64,3584]{1,0:T(8,128)(2,1)}), bf16[1024,3584]{1,0:T(8,128)(2,1)}) %all-gather.5.cloned.1.call-update) | async-done | bytes 7340048 | tf_op jit(solution)/shard_map/all_gather | solution.py:59
  156.5 0.0 copy-done.3
  156.5 0.0 copy-start.1
  156.5 5.5 %fusion.4 = f32[1024,64]{0,1:T(8,128)S(1)} fusion(bf16[1024,3584]{1,0:T(8,128)(2,1)} %all-gather.5.cloned.1.call-done, bf16[1,64,3584]{2,1,0:T(8,128)(2,1)S(1)} %copy-done.3), kind=kOutput, calls=%fused_computation.9 | convolution fusion | flops 469762048 | bytes 8060928 | tf_op jit(solution)/shard_map/dot_general | solution.py:11
  162.1 0.0 copy-done.4
  162.1 0.0 copy-done.1
  162.1 2.3 fusion.6
  164.4 106.6 %all-gather.3.cloned.1.call-done = bf16[1024,3584]{1,0:T(8,128)(2,1)} async-done(((bf16[64,3584]{1,0:T(8,128)(2,1)}), bf16[1024,3584]{1,0:T(8,128)(2,1)}) %all-gather.3.cloned.1.call-update) | async-done | bytes 7340048 | tf_op jit(solution)/shard_map/all_gather | solution.py:60
  271.0 0.0 copy-done.5
  271.0 0.0 copy-start.2
  271.0 5.5 %fusion.8 = f32[1024,64]{0,1:T(8,128)S(1)} fusion(bf16[1024,3584]{1,0:T(8,128)(2,1)} %all-gather.3.cloned.1.call-done, bf16[1,64,3584]{2,1,0:T(8,128)(2,1)S(1)} %copy-done.5), kind=kOutput, calls=%fused_computation.13 | convolution fusion | flops 469762048 | bytes 8060928 | tf_op jit(solution)/shard_map/dot_general | solution.py:13
  276.6 0.0 copy-done.2
  276.6 0.0 slice-start
  276.6 2.1 fusion.3
  278.7 0.0 slice-start.1
  278.7 5.4 %fusion.1 = bf16[1,64,3584]{2,1,0:T(8,128)(2,1)} fusion(bf16[1024,3584]{1,0:T(8,128)(2,1)} %all-gather.5.cloned.1.call-done, f32[1024,64]{0,1:T(8,128)S(1)} %fusion.4, f32[1024,64]{0,1:T(8,128)S(1)} %fusion.8, f32[1024,64]{0,1:T(8,128)S(1)} %fusion.6), kind=kOutput, calls=%fused_computation.6 | convolution fusion | flops 470646784 | bytes 8585216 | tf_op jit(solution)/shard_map/dot_general | solution.py:25
  284.1 0.0 slice-done
  284.1 0.0 slice-done.1
  284.1 2.1 fusion.2
  (6 shorter events, 0.1 us)
Async XLA Ops:
  7.2 12.8 %copy-start = (bf16[128,3584]{1,0:T(8,128)(2,1)S(1)}, bf16[128,3584]{1,0:T(8,128)(2,1)}, u32[]{:S(2)}) copy-start(bf16[128,3584]{1,0:T(8,128)(2,1)} %param.7) | copy-start | bytes 2752516
  7.2 149.3 %copy-start.3 = (bf16[1,64,3584]{2,1,0:T(8,128)(2,1)S(1)}, bf16[1,64,3584]{2,1,0:T(8,128)(2,1)}, u32[]{:S(2)}) copy-start(bf16[1,64,3584]{2,1,0:T(8,128)(2,1)} %param.11) | copy-start | bytes 1376260
  7.2 149.3 %all-gather.5.cloned.1.call-start = ((), (), s32[]{:S(2)}) async-start(), calls=%async_computation.3 | async-start | bytes 7798784 | tf_op jit(solution)/shard_map/all_gather | solution.py:59
  47.5 114.6 %copy-start.4 = (bf16[1,64,3584]{2,1,0:T(8,128)(2,1)S(1)}, bf16[1,64,3584]{2,1,0:T(8,128)(2,1)}, u32[]{:S(2)}) copy-start(bf16[1,64,3584]{2,1,0:T(8,128)(2,1)} %param.12) | copy-start | bytes 1376260
  48.4 222.6 %all-gather.3.cloned.1.call-start = ((), (), s32[]{:S(2)}) async-start(), calls=%async_computation.2 | async-start | bytes 7798784 | tf_op jit(solution)/shard_map/all_gather | solution.py:60
  70.6 200.4 %copy-start.5 = (bf16[1,64,3584]{2,1,0:T(8,128)(2,1)S(1)}, bf16[1,64,3584]{2,1,0:T(8,128)(2,1)}, u32[]{:S(2)}) copy-start(bf16[1,64,3584]{2,1,0:T(8,128)(2,1)} %param.13) | copy-start | bytes 1376260
  156.5 5.6 %copy-start.1 = (bf16[1024,3584]{1,0:T(8,128)(2,1)S(1)}, bf16[1024,3584]{1,0:T(8,128)(2,1)}, u32[]{:S(2)}) copy-start(bf16[1024,3584]{1,0:T(8,128)(2,1)} %all-gather.5.cloned.1.call-done) | copy-start | bytes 22020100
  271.0 5.5 %copy-start.2 = (bf16[1024,3584]{1,0:T(8,128)(2,1)S(1)}, bf16[1024,3584]{1,0:T(8,128)(2,1)}, u32[]{:S(2)}) copy-start(bf16[1024,3584]{1,0:T(8,128)(2,1)} %all-gather.3.cloned.1.call-done) | copy-start | bytes 22020100
  276.6 7.5 %slice-start = ((s8[7340032]{0:T(1024)(128)(4,1)}), s8[4194304]{0:T(1024)(128)(4,1)S(1)}, s32[]{:S(2)}) async-start(s8[7340032]{0:T(1024)(128)(4,1)} %bitcast.43), calls=%async_computation.4 | async-start | bytes 8388608
  278.7 5.4 %slice-start.1 = ((s8[7340032]{0:T(1024)(128)(4,1)}), s8[3145728]{0:T(1024)(128)(4,1)S(1)}, s32[]{:S(2)}) async-start(s8[7340032]{0:T(1024)(128)(4,1)} %bitcast.43), calls=%async_computation.5 | async-start | bytes 6291456
Sparse Core Ops, SparseCore 0:
  48.6 107.9 all-gather.4
  160.1 110.8 all-gather.2
where the time goes:
time: 293 us
  waiting for transfers between devices  193 us (66%)
  blocking collectives  46.6 us (16%)
  matrix products  24.7 us (8%)
  between operations  14.2 us (5%)
  other arithmetic  11.2 us (4%)
  local copies, waits for them, and re-layouts  3.76 us (1%)
    all_gather x1, waiting for transfers between devices, local(): piece_dy = lax.all_gather(rows_dy, 'dp', axis=0, tiled=True)  107 us
    all_gather x1, waiting for transfers between devices, local(): piece_x = lax.all_gather(rows_x, 'dp', axis=0, tiled=True)  85.9 us
    all_to_all x1, blocking collectives, local(): lax.all_to_all(sent_x, 'expert', split_axis=0, concat_axis=0, tiled=True)  27.1 us
    all_to_all x1, blocking collectives, local(): lax.all_to_all(sent_dy, 'expert', split_axis=0, concat_axis=0, tiled=True)  19.5 us
    dot_general x3, matrix products, outer_sum(): lax.dot_general(factor, rows, (((0,), (0,)), ((), ())), preferred_element...  9.65 us
    another operation x3, other arithmetic  9.15 us
  transfers between devices with their start and end apart: 2, of which 2 were waited for; matrix products, arithmetic and copies ran while one was open for 4% of the time, Pallas kernels for 0%

commit v1 on v0

--- a/solution.py
+++ b/solution.py
@@ -57,7 +57,10 @@
     rows_x = recv_x.reshape(-1, feature_count)
     rows_dy = recv_dy.reshape(-1, feature_count)
     piece_x = lax.all_gather(rows_x, "dp", axis=0, tiled=True)
-    piece_dy = lax.all_gather(rows_dy, "dp", axis=0, tiled=True)
+    a_now = lax.axis_size("dp")
+    local_part = jnp.stack(a_now * [rows_dy], axis=0)
+    r1 = lax.all_to_all(local_part, "dp", 0, 0)
+    piece_dy = jnp.concatenate(r1, axis=0)
     d_gate, d_up, hidden = local_factors(piece_x, piece_dy, w_gate[0], w_up[0], w_down[0])
     term_gate = outer_sum(d_gate, piece_x)
     term_up = outer_sum(d_up, piece_x)

time: 293 us -> 352 us (1.20)
  the two profiles are of different devices: /device:TPU:1 before, /device:TPU:493 now
where the time goes in v1:
time: 352 us
  waiting for transfers between devices  271 us (77%)
  matrix products  24.5 us (7%)
  starting transfers between devices  22.4 us (6%)
  between operations  14.2 us (4%)
  other arithmetic  11.2 us (3%)
  local copies, waits for them, and re-layouts  8.22 us (2%)
    all_to_all x1, waiting for transfers between devices, local(): r1 = lax.all_to_all(local_part, 'dp', 0, 0)  249 us
    all_to_all x1, waiting for transfers between devices, local(): lax.all_to_all(sent_x, 'expert', split_axis=0, concat_axis=0, tiled=True)  12.3 us
    all_to_all x1, waiting for transfers between devices, local(): lax.all_to_all(sent_dy, 'expert', split_axis=0, concat_axis=0, tiled=True)  10.1 us
    dot_general x3, matrix products, outer_sum(): lax.dot_general(factor, rows, (((0,), (0,)), ((), ())), preferred_element...  9.49 us
    all_to_all x1, starting transfers between devices, local(): r1 = lax.all_to_all(local_part, 'dp', 0, 0)  9.2 us
    another operation x3, other arithmetic  9.15 us
    all_to_all x1, starting transfers between devices, local(): lax.all_to_all(sent_x, 'expert', split_axis=0, concat_axis=0, tiled=True)  7.26 us
  transfers between devices with their start and end apart: 4, of which 3 were waited for; matrix products, arithmetic and copies ran while one was open for 3% of the time, Pallas kernels for 0%

profile of v1, /device:TPU:493, one launch (start us, length us, event | category | flops | bytes accessed | tf_op | source)
XLA Modules:
  0.0 351.9 jit_solution(14152359529279201841)
XLA Ops:
  7.2 0.0 copy-start
  7.2 0.9 copy.30
  8.0 0.1 eq.43
  8.1 0.1 eq.39
  8.3 9.0 %reduce-window.6 = s32[32,8,128]{2,1,0:T(8,128)S(1)} reduce-window(s32[32,8,128]{2,1,0:T(8,128)S(1)} %fusion.15, s32[]{:T(128)} %constant.4.clone.1), window={size=1x1x128 pad=0_0x0_0x127_0}, to_apply=%region_0.0 | reduce-window | flops 4161536 | bytes 262148 | tf_op jit(solution)/shard_map/reduce-window
  17.3 0.1 slice.8
  17.4 0.1 copy.32
  17.5 0.1 copy.33
  17.6 0.1 broadcast_add_fusion
  17.8 0.1 reduce_sum.30
  17.9 0.7 add_select_fusion
  18.6 1.2 select_reduce_fusion
  19.9 0.0 copy-done
  19.9 0.3 fusion
  20.1 0.9 reshape.64
  21.1 5.9 %all-to-all-start = ((bf16[32,2,3584]{2,1,0:T(2,128)(2,1)}), bf16[32,2,3584]{2,1,0:T(2,128)(2,1)S(1)}, u32[]{:S(2)}, u32[]{:S(2)}) async-start(bf16[32,2,3584]{2,1,0:T(2,128)(2,1)} %reshape.64), calls=%async_computation | async-start | bytes 917504 | tf_op jit(solution)/shard_map/all_to_all | solution.py:55
  27.0 1.4 convolution_convert_fusion.3
  28.5 0.9 reshape.66
  29.4 10.1 %all-to-all-done = bf16[32,2,3584]{2,1,0:T(2,128)(2,1)S(1)} async-done(((bf16[32,2,3584]{2,1,0:T(2,128)(2,1)}), bf16[32,2,3584]{2,1,0:T(2,128)(2,1)S(1)}, u32[]{:S(2)}, u32[]{:S(2)}) %all-to-all-start) | async-done | bytes 458784 | tf_op jit(solution)/shard_map/all_to_all | solution.py:55
  39.5 7.3 %all-to-all-start.2 = ((bf16[32,2,3584]{2,1,0:T(2,128)(2,1)}), bf16[32,2,3584]{2,1,0:T(2,128)(2,1)S(1)}, u32[]{:S(2)}, u32[]{:S(2)}) async-start(bf16[32,2,3584]{2,1,0:T(2,128)(2,1)} %reshape.66), calls=%async_computation.2 | async-start | bytes 917504 | tf_op jit(solution)/shard_map/all_to_all | solution.py:54
  46.8 0.2 stack_reshape.2
  46.9 12.3 %all-to-all-done.2 = bf16[32,2,3584]{2,1,0:T(2,128)(2,1)S(1)} async-done(((bf16[32,2,3584]{2,1,0:T(2,128)(2,1)}), bf16[32,2,3584]{2,1,0:T(2,128)(2,1)S(1)}, u32[]{:S(2)}, u32[]{:S(2)}) %all-to-all-start.2) | async-done | bytes 458784 | tf_op jit(solution)/shard_map/all_to_all | solution.py:54
  59.2 3.7 %stack.3 = bf16[16,64,3584]{2,1,0:T(8,128)(2,1)} broadcast(bf16[64,3584]{1,0:T(8,128)(2,1)S(1)} %stack_reshape.2), dimensions={1,2} | broadcast | bytes 7798784 | tf_op jit(solution)/shard_map/stack | solution.py:61
  63.0 0.0 copy-start.2
  63.0 9.2 %all-to-all-start.1 = ((bf16[16,64,3584]{2,1,0:T(8,128)(2,1)}), bf16[16,64,3584]{2,1,0:T(8,128)(2,1)}, u32[]{:S(2)}, u32[]{:S(2)}) async-start(bf16[16,64,3584]{2,1,0:T(8,128)(2,1)} %stack.3), calls=%async_computation.1 | async-start | bytes 14680064 | tf_op jit(solution)/shard_map/all_to_all | solution.py:62
  72.2 0.0 copy-start.3
  72.2 0.0 all-gather.2.cloned.1.call-start
  72.2 0.9 reshape.67
  73.2 0.0 all-gather.2.cloned.1.call-update
  73.2 249.0 %all-to-all-done.1 = bf16[16,64,3584]{2,1,0:T(8,128)(2,1)} async-done(((bf16[16,64,3584]{2,1,0:T(8,128)(2,1)}), bf16[16,64,3584]{2,1,0:T(8,128)(2,1)}, u32[]{:S(2)}, u32[]{:S(2)}) %all-to-all-start.1) | async-done | bytes 7340064 | tf_op jit(solution)/shard_map/all_to_all | solution.py:62
  322.2 0.0 copy-done.2
  322.2 0.0 copy-start.4
  322.2 5.4 %fusion.8 = f32[1024,64]{0,1:T(8,128)S(1)} fusion(bf16[1024,3584]{1,0:T(8,128)(2,1)} %bitcast.2, bf16[1,64,3584]{2,1,0:T(8,128)(2,1)S(1)} %copy-done.2), kind=kOutput, calls=%fused_computation.13 | convolution fusion | flops 469762048 | bytes 8060928 | tf_op jit(solution)/shard_map/dot_general | solution.py:13
  327.7 0.0 all-gather.2.cloned.1.call-done
  327.7 0.0 copy-done.3
  327.7 0.0 copy-start.1
  327.7 5.5 %fusion.4 = f32[1024,64]{0,1:T(8,128)S(1)} fusion(bf16[1024,3584]{1,0:T(8,128)(2,1)} %all-gather.2.cloned.1.call-done, bf16[1,64,3584]{2,1,0:T(8,128)(2,1)S(1)} %copy-done.3), kind=kOutput, calls=%fused_computation.9 | convolution fusion | flops 469762048 | bytes 8060928 | tf_op jit(solution)/shard_map/dot_general | solution.py:11
  333.3 0.0 copy-done.4
  333.3 0.0 copy-done.1
  333.3 2.3 fusion.6
  335.6 5.2 %fusion.3 = bf16[1,64,3584]{2,1,0:T(8,128)(2,1)} fusion(bf16[1024,3584]{1,0:T(8,128)(2,1)} %bitcast.2, f32[1024,64]{0,1:T(8,128)S(1)} %fusion.6, f32[1024,64]{0,1:T(8,128)S(1)} %fusion.4), kind=kOutput, calls=%fused_computation.8 | convolution fusion | flops 470384640 | bytes 8323072 | tf_op jit(solution)/shard_map/dot_general | solution.py:25
  340.8 2.2 fusion.1
  343.0 2.1 fusion.2
  (5 shorter events, 0.1 us)
Async XLA Ops:
  7.2 12.7 %copy-start = (bf16[128,3584]{1,0:T(8,128)(2,1)S(1)}, bf16[128,3584]{1,0:T(8,128)(2,1)}, u32[]{:S(2)}) copy-start(bf16[128,3584]{1,0:T(8,128)(2,1)} %param.10) | copy-start | bytes 2752516
  21.1 18.4 %all-to-all-start = ((bf16[32,2,3584]{2,1,0:T(2,128)(2,1)}), bf16[32,2,3584]{2,1,0:T(2,128)(2,1)S(1)}, u32[]{:S(2)}, u32[]{:S(2)}) async-start(bf16[32,2,3584]{2,1,0:T(2,128)(2,1)} %reshape.64), calls=%async_computation | async-start | bytes 917504 | tf_op jit(solution)/shard_map/all_to_all | solution.py:55
  39.5 19.7 %all-to-all-start.2 = ((bf16[32,2,3584]{2,1,0:T(2,128)(2,1)}), bf16[32,2,3584]{2,1,0:T(2,128)(2,1)S(1)}, u32[]{:S(2)}, u32[]{:S(2)}) async-start(bf16[32,2,3584]{2,1,0:T(2,128)(2,1)} %reshape.66), calls=%async_computation.2 | async-start | bytes 917504 | tf_op jit(solution)/shard_map/all_to_all | solution.py:54
  63.0 259.3 %copy-start.2 = (bf16[1,64,3584]{2,1,0:T(8,128)(2,1)S(1)}, bf16[1,64,3584]{2,1,0:T(8,128)(2,1)}, u32[]{:S(2)}) copy-start(bf16[1,64,3584]{2,1,0:T(8,128)(2,1)} %param.13) | copy-start | bytes 1376260
  63.0 259.3 %all-to-all-start.1 = ((bf16[16,64,3584]{2,1,0:T(8,128)(2,1)}), bf16[16,64,3584]{2,1,0:T(8,128)(2,1)}, u32[]{:S(2)}, u32[]{:S(2)}) async-start(bf16[16,64,3584]{2,1,0:T(8,128)(2,1)} %stack.3), calls=%async_computation.1 | async-start | bytes 14680064 | tf_op jit(solution)/shard_map/all_to_all | solution.py:62
  72.2 255.5 %copy-start.3 = (bf16[1,64,3584]{2,1,0:T(8,128)(2,1)S(1)}, bf16[1,64,3584]{2,1,0:T(8,128)(2,1)}, u32[]{:S(2)}) copy-start(bf16[1,64,3584]{2,1,0:T(8,128)(2,1)} %param.11) | copy-start | bytes 1376260
  72.2 255.5 %all-gather.2.cloned.1.call-start = ((), (), s32[]{:S(2)}) async-start(), calls=%async_computation.3 | async-start | bytes 7798784 | tf_op jit(solution)/shard_map/all_gather | solution.py:59
  322.2 11.0 %copy-start.4 = (bf16[1,64,3584]{2,1,0:T(8,128)(2,1)S(1)}, bf16[1,64,3584]{2,1,0:T(8,128)(2,1)}, u32[]{:S(2)}) copy-start(bf16[1,64,3584]{2,1,0:T(8,128)(2,1)} %param.12) | copy-start | bytes 1376260
  327.7 5.6 %copy-start.1 = (bf16[1024,3584]{1,0:T(8,128)(2,1)S(1)}, bf16[1024,3584]{1,0:T(8,128)(2,1)}, u32[]{:S(2)}) copy-start(bf16[1024,3584]{1,0:T(8,128)(2,1)} %all-gather.2.cloned.1.call-done) | copy-start | bytes 22020100
Sparse Core Ops, SparseCore 0:
  76.6 229.6 all-gather.1
